TPU v7x, 512 devices: a whole 4x4x16 slice. The times are simulated.
512 devices in a mesh: shard: 64 (over z, x), tensor: 4 (over y), section: 2 (over core).
Axes of the slice: x: 4, y: 4, z: 16, core: 2. Of those that a mesh axis runs over, the one named last changes fastest.
Arguments:
- query_key: float32 [2, 2, 1024, 1024], P('section', None, 'shard', 'tensor'), may hold values from -52 to 52, as said below
- query_key_gradient: float32 [2, 2, 1024, 1024], P('section', None, 'shard', 'tensor'), may hold values from -52 to 52
- query_key_first: float32 [2, 2, 1024, 1024], P('section', None, 'shard', 'tensor'), may hold values from -5.2 to 5.2
- query_key_second: float32 [2, 2, 1024, 1024], P('section', None, 'shard', 'tensor'), may hold values from 0.01 to 1
- value_gate: float32 [2, 2, 1024, 2048], P('section', None, 'shard', 'tensor'), may hold values from -52 to 52
- value_gate_gradient: float32 [2, 2, 1024, 2048], P('section', None, 'shard', 'tensor'), may hold values from -52 to 52
- value_gate_first: float32 [2, 2, 1024, 2048], P('section', None, 'shard', 'tensor'), may hold values from -5.2 to 5.2
- value_gate_second: float32 [2, 2, 1024, 2048], P('section', None, 'shard', 'tensor'), may hold values from 0.01 to 1
- output_weight: float32 [2, 2048, 1024], P('section', 'tensor', 'shard'), may hold values from -52 to 52
- output_gradient: float32 [2, 2048, 1024], P('section', 'tensor', 'shard'), may hold values from -52 to 52
- output_first: float32 [2, 2048, 1024], P('section', 'tensor', 'shard'), may hold values from -5.2 to 5.2
- output_second: float32 [2, 2048, 1024], P('section', 'tensor', 'shard'), may hold values from 0.01 to 1
- norm_gain: float32 [2, 1024], P('section', 'shard'), may hold values from -52 to 52
- gain_gradient: float32 [2, 1024], P('section', 'shard'), may hold values from -52 to 52
- gain_first: float32 [2, 1024], P('section', 'shard'), may hold values from -5.2 to 5.2
- gain_second: float32 [2, 1024], P('section', 'shard'), may hold values from 0.01 to 1
Outputs:
- new_query_key: float32 [2, 2, 1024, 1024], P('section', None, 'shard', 'tensor')
- new_query_key_first: float32 [2, 2, 1024, 1024], P('section', None, 'shard', 'tensor')
- new_query_key_second: float32 [2, 2, 1024, 1024], P('section', None, 'shard', 'tensor')
- new_value_gate: float32 [2, 2, 1024, 2048], P('section', None, 'shard', 'tensor')
- new_value_gate_first: float32 [2, 2, 1024, 2048], P('section', None, 'shard', 'tensor')
- new_value_gate_second: float32 [2, 2, 1024, 2048], P('section', None, 'shard', 'tensor')
- new_output: float32 [2, 2048, 1024], P('section', 'tensor', 'shard')
- new_output_first: float32 [2, 2048, 1024], P('section', 'tensor', 'shard')
- new_output_second: float32 [2, 2048, 1024], P('section', 'tensor', 'shard')
- new_gain: float32 [2, 1024], P('section', 'shard')
- new_gain_first: float32 [2, 1024], P('section', 'shard')
- new_gain_second: float32 [2, 1024], P('section', 'shard')
- copy_query_key: bfloat16 [2, 2, 1024, 1024], P('section', None, None, 'tensor')
- copy_value_gate: bfloat16 [2, 2, 1024, 2048], P('section', None, None, 'tensor')
- copy_output: bfloat16 [2, 2048, 1024], P('section', 'tensor')
- copy_gain: bfloat16 [2, 1024], P('section')
Inputs may be any that keep to these rules, and one draw needn't show every extreme that they name: `query_key`: projection weights, gradients and first moments are real-valued with entries of differing scale.
All inputs are finite; a program needn't handle non-finite values.
Results may differ from a plain program's by a relative error of at most 0.001.
Values may be sent and summed in bfloat16 or wider, within the bound.
A program may use at most 64 MiB of HBM per device.

v0:
```python
import jax
import jax.numpy as jnp
from jax import lax
from jax.sharding import PartitionSpec as P

STEP = 10


beta_one = 0.9
beta_two = 0.999
epsilon = 1e-06
learn_rate = 0.2


def local_terms(weight, gradient, first, second, decay, matrix_dims):
    first_new = beta_one * first + (1.0 - beta_one) * gradient
    second_new = beta_two * second + (1.0 - beta_two) * gradient * gradient
    update = (
        first_new
        / (1.0 - beta_one**STEP)
        / (jnp.sqrt(second_new / (1.0 - beta_two**STEP)) + epsilon)
        + decay * weight
    )
    norm_axes = tuple(range(weight.ndim - matrix_dims, weight.ndim))
    weight_sq = jnp.sum(weight * weight, axis=norm_axes)
    update_sq = jnp.sum(update * update, axis=norm_axes)
    return (first_new, second_new, update, weight_sq, update_sq)


def apply_trust(weight, update, weight_sq, update_sq, matrix_dims):
    trust = jnp.sqrt(weight_sq) / (jnp.sqrt(update_sq) + epsilon)
    trust = trust.reshape(trust.shape + (1,) * matrix_dims)
    return weight - learn_rate * trust * update


def on_device(
    query_key,
    query_key_gradient,
    query_key_first,
    query_key_second,
    value_gate,
    value_gate_gradient,
    value_gate_first,
    value_gate_second,
    output_weight,
    output_gradient,
    output_first,
    output_second,
    norm_gain,
    gain_gradient,
    gain_first,
    gain_second,
):
    qk_terms = local_terms(
        query_key, query_key_gradient, query_key_first, query_key_second, 0.01, 2
    )
    vg_terms = local_terms(
        value_gate, value_gate_gradient, value_gate_first, value_gate_second, 0.01, 2
    )
    output_terms = local_terms(output_weight, output_gradient, output_first, output_second, 0.01, 2)
    gain_terms = local_terms(norm_gain, gain_gradient, gain_first, gain_second, 0.0, 1)
    qk_sq = lax.psum((qk_terms[3], qk_terms[4]), ("shard", "tensor"))
    vg_sq = lax.psum((vg_terms[3], vg_terms[4]), ("shard", "tensor"))
    output_sq = lax.psum((output_terms[3], output_terms[4]), ("shard", "tensor"))
    gain_sq = lax.psum((gain_terms[3], gain_terms[4]), "shard")
    new_qk = apply_trust(query_key, qk_terms[2], qk_sq[0], qk_sq[1], 2)
    new_vg = apply_trust(value_gate, vg_terms[2], vg_sq[0], vg_sq[1], 2)
    new_output = apply_trust(output_weight, output_terms[2], output_sq[0], output_sq[1], 2)
    new_gain = apply_trust(norm_gain, gain_terms[2], gain_sq[0], gain_sq[1], 1)
    qk_half = new_qk.astype(jnp.bfloat16)
    vg_half = new_vg.astype(jnp.bfloat16)
    output_half = new_output.astype(jnp.bfloat16)
    gain_half = new_gain.astype(jnp.bfloat16)
    copy_qk = lax.all_gather(qk_half, "shard", axis=2, tiled=True)
    copy_vg = lax.all_gather(vg_half, "shard", axis=2, tiled=True)
    copy_output = lax.all_gather(output_half, "shard", axis=2, tiled=True)
    copy_gain = lax.all_gather(gain_half, "shard", axis=1, tiled=True)
    return (
        new_qk,
        qk_terms[0],
        qk_terms[1],
        new_vg,
        vg_terms[0],
        vg_terms[1],
        new_output,
        output_terms[0],
        output_terms[1],
        new_gain,
        gain_terms[0],
        gain_terms[1],
        copy_qk,
        copy_vg,
        copy_output,
        copy_gain,
    )


def solution(mesh):
    placed = (
        P("section", None, "shard", "tensor"),
        P("section", None, "shard", "tensor"),
        P("section", None, "shard", "tensor"),
        P("section", None, "shard", "tensor"),
        P("section", None, "shard", "tensor"),
        P("section", None, "shard", "tensor"),
        P("section", None, "shard", "tensor"),
        P("section", None, "shard", "tensor"),
        P("section", "tensor", "shard"),
        P("section", "tensor", "shard"),
        P("section", "tensor", "shard"),
        P("section", "tensor", "shard"),
        P("section", "shard"),
        P("section", "shard"),
        P("section", "shard"),
        P("section", "shard"),
    )
    return jax.shard_map(
        on_device,
        mesh=mesh,
        in_specs=placed,
        out_specs=(
            P("section", None, "shard", "tensor"),
            P("section", None, "shard", "tensor"),
            P("section", None, "shard", "tensor"),
            P("section", None, "shard", "tensor"),
            P("section", None, "shard", "tensor"),
            P("section", None, "shard", "tensor"),
            P("section", "tensor", "shard"),
            P("section", "tensor", "shard"),
            P("section", "tensor", "shard"),
            P("section", "shard"),
            P("section", "shard"),
            P("section", "shard"),
            P("section", None, None, "tensor"),
            P("section", None, None, "tensor"),
            P("section", "tensor", None),
            P("section", None),
        ),
        check_vma=False,
    )
```

profile of v0, /device:TPU:1, one launch (start us, length us, event | category | flops | bytes accessed | tf_op | source)
XLA Modules:
  0.0 1112.5 jit_solution(3101346954064736465)
XLA Ops:
  7.2 0.0 all-gather.4.cloned.1.call-start
  7.2 1.1 multiply_reduce_fusion.1
  8.3 1.0 multiply_reduce_fusion.5
  9.3 1.5 multiply_reduce_fusion.2
  10.8 588.4 %all-reduce.1 = (f32[1,2]{1,0:T(1,128)S(1)}, f32[1,2]{1,0:T(1,128)S(1)}, f32[1,2]{1,0:T(1,128)S(1)}, f32[1,2]{1,0:T(1,128)S(1)}, f32[1]{0:T(128)}, /*index=5*/f32[1]{0:T(128)}) all-reduce(f32[1,2]{1,0:T(1,128)S(1)} %bitcast.20, f32[1,2]{1,0:T(1,128)S(1)} %bitcast.19, ...), channel_id=1, replica_groups=mesh['shard'=64,'tensor'=4,'section'=2] {'shard','tensor'}, use_global_device_ids=true, to_apply=%region_3.0 | all-reduce | flops 10 | bytes 80 | tf_op jit(solution)/shard_map/psum | solution.py:62
  599.2 1.5 fusion.6
  600.6 0.0 all-gather.4.cloned.1.call-update
  600.7 0.0 all-gather.8.cloned.1.call-start
  602.1 1.4 fusion.4
  603.5 0.0 all-gather.6.cloned.1.call-start
  603.6 1.6 fusion.5
  605.2 1.8 multiply_reduce_fusion.6
  607.0 111.7 %all-reduce.2 = (f32[1]{0:T(128)}, f32[1]{0:T(128)}) all-reduce(f32[1]{0:T(128)} %bitcast.9, f32[1]{0:T(128)} %bitcast.10), channel_id=1, replica_groups=mesh['shard'=64,'tensor'=4,'section'=2] {'shard'}, use_global_device_ids=true, to_apply=%region_13.0 | all-reduce | flops 2 | bytes 16 | tf_op jit(solution)/shard_map/psum | solution.py:65
  720.1 1.3 dynamic-slice
  722.0 1.2 convert_bitcast_fusion
  723.2 0.2 dynamic-update-slice
  723.4 112.1 %all-reduce = bf16[1024]{0:T(1024)(128)(2,1)S(1)} all-reduce(bf16[1024]{0:T(1024)(128)(2,1)S(1)} %dynamic-update-slice), channel_id=1, replica_groups=mesh['shard'=64,'tensor'=4,'section'=2] {'shard'}, use_global_device_ids=true, to_apply=%add | all-reduce | flops 1024 | bytes 4096
  835.5 0.6 reshape.78
  836.1 125.4 %all-gather.8.cloned.1.call-done = bf16[1,512,1024]{1,2,0:T(8,128)(2,1)} async-done(((bf16[1,512,16]{1,2,0:T(8,128)(2,1)}), bf16[1,512,1024]{1,2,0:T(8,128)(2,1)}) %all-gather.8.cloned.1.call-update) | async-done | bytes 1048592 | tf_op jit(solution)/shard_map/all_gather | solution.py:76
  961.5 2.3 copy.33
  963.7 139.0 %all-gather.6.cloned.1.call-done = bf16[1,2,1024,512]{3,2,1,0:T(8,128)(2,1)} async-done(((bf16[1,2,16,512]{3,2,1,0:T(8,128)(2,1)}), bf16[1,2,1024,512]{3,2,1,0:T(8,128)(2,1)}) %all-gather.6.cloned.1.call-update) | async-done | bytes 2097168 | tf_op jit(solution)/shard_map/all_gather | solution.py:75
  1102.7 1.0 copy.37
  1103.7 1.0 copy-done
  1104.7 1.3 copy.38
  (20 shorter events, 0.1 us)
Async XLA Ops:
  7.2 828.9 %all-gather.4.cloned.1.call-start = ((), (), s32[]{:S(2)}) async-start(), calls=%async_computation | async-start | bytes 1064960 | tf_op jit(solution)/shard_map/all_gather | solution.py:74
  8.3 1095.4 %copy-start.2 = (f32[1,2,16,512]{3,2,1,0:T(8,128)}, f32[1,2,16,512]{3,2,1,0:T(8,128)S(1)}, u32[]{:S(2)}) copy-start(f32[1,2,16,512]{3,2,1,0:T(8,128)S(1)} %get-tuple-element.87) | copy-start | bytes 196612
  8.3 1095.4 %copy-start.3 = (f32[1,2,16,512]{3,2,1,0:T(8,128)}, f32[1,2,16,512]{3,2,1,0:T(8,128)S(1)}, u32[]{:S(2)}) copy-start(f32[1,2,16,512]{3,2,1,0:T(8,128)S(1)} %get-tuple-element.88) | copy-start | bytes 196612
  9.3 1094.4 %copy-start.4 = (f32[1,2,16,256]{3,2,1,0:T(8,128)}, f32[1,2,16,256]{3,2,1,0:T(8,128)S(1)}, u32[]{:S(2)}) copy-start(f32[1,2,16,256]{3,2,1,0:T(8,128)S(1)} %get-tuple-element.84) | copy-start | bytes 98308
  9.3 1094.4 %copy-start.5 = (f32[1,2,16,256]{3,2,1,0:T(8,128)}, f32[1,2,16,256]{3,2,1,0:T(8,128)S(1)}, u32[]{:S(2)}) copy-start(f32[1,2,16,256]{3,2,1,0:T(8,128)S(1)} %get-tuple-element.85) | copy-start | bytes 98308
  10.8 1092.9 %copy-start.6 = (f32[1,512,16]{1,2,0:T(8,128)}, f32[1,512,16]{1,2,0:T(8,128)S(1)}, u32[]{:S(2)}) copy-start(f32[1,512,16]{1,2,0:T(8,128)S(1)} %get-tuple-element.90) | copy-start | bytes 98308
  10.8 1092.9 %copy-start.7 = (f32[1,512,16]{1,2,0:T(8,128)}, f32[1,512,16]{1,2,0:T(8,128)S(1)}, u32[]{:S(2)}) copy-start(f32[1,512,16]{1,2,0:T(8,128)S(1)} %get-tuple-element.91) | copy-start | bytes 98308
  600.7 360.8 %all-gather.8.cloned.1.call-start = ((), (), s32[]{:S(2)}) async-start(), calls=%async_computation.2 | async-start | bytes 1064960 | tf_op jit(solution)/shard_map/all_gather | solution.py:76
  603.5 499.2 %all-gather.6.cloned.1.call-start = ((), (), s32[]{:S(2)}) async-start(), calls=%async_computation.1 | async-start | bytes 2129920 | tf_op jit(solution)/shard_map/all_gather | solution.py:75
  836.1 266.6 %copy-start.1 = (bf16[1,2,1024,256]{3,2,1,0:T(8,128)(2,1)S(1)}, bf16[1,2,1024,256]{3,2,1,0:T(8,128)(2,1)}, u32[]{:S(2)}) copy-start(bf16[1,2,1024,256]{3,2,1,0:T(8,128)(2,1)} %all-gather.4.cloned.1.call-done) | copy-start | bytes 3145732
  1102.7 2.0 copy-start
Sparse Core Ops, SparseCore 0:
  600.8 222.2 all-gather.3
  826.5 134.8 all-gather.7
  965.0 137.6 all-gather.5
where the time goes:
time: 1120 us; the launch traced here: 1110 us
  blocking collectives  812 us (72%)
  waiting for transfers between devices  264 us (24%)
  between operations  17.3 us (2%)
    psum x1, blocking collectives, on_device(): qk_sq = lax.psum((qk_terms[3], qk_terms[4]), ('shard', 'tensor'))  588 us
    all_gather x1, waiting for transfers between devices, on_device(): copy_vg = lax.all_gather(vg_half, 'shard', axis=2, tiled=True)  139 us
    all_gather x1, waiting for transfers between devices, on_device(): copy_output = lax.all_gather(output_half, 'shard', axis=2, tiled=True)  125 us
    unnamed x1, blocking collectives  112 us
    psum x1, blocking collectives, on_device(): gain_sq = lax.psum((gain_terms[3], gain_terms[4]), 'shard')  112 us
  transfers between devices with their start and end apart: 3, of which 2 were waited for; matrix products, arithmetic and copies ran while one was open for 1% of the time, Pallas kernels for 0%

commit v1 on v0

v1 whole, which is shorter than its diff:
```python
import functools

import jax
import jax.numpy as jnp
from jax import lax
from jax.experimental import pallas as pl
from jax.experimental.pallas import tpu as pltpu
from jax.sharding import PartitionSpec as P

STEP = 10
BETA_ONE = 0.9
BETA_TWO = 0.999
EPSILON = 1e-06
LEARN_RATE = 0.2
FIRST_SCALE = 1.0 / (1.0 - BETA_ONE**STEP)
SECOND_SCALE = 1.0 / (1.0 - BETA_TWO**STEP)

MESH = pl.DeviceIdType.MESH
NX, NY, NZ = 4, 4, 16
HALF = NZ // 2
ROWS = 16
GROUP = NX * ROWS
A_COLS, B_COLS = 768, 1280
SUBS = 4
W_LANE, U_LANE = 64, 72
LAG = 1


def terms(p, g, m, s, decay):
    first = BETA_ONE * m + (1.0 - BETA_ONE) * g
    second = BETA_TWO * s + (1.0 - BETA_TWO) * g * g
    update = first * FIRST_SCALE / (jnp.sqrt(second * SECOND_SCALE) + EPSILON)
    if decay:
        update = update + decay * p
    return first, second, update


def total(v):
    return jnp.sum(jnp.sum(v, axis=0, keepdims=True), axis=1, keepdims=True)


def comm_kernel(*refs):
    (qk_p, qk_g, qk_m, qk_s, vg_p, vg_g, vg_m, vg_s, o_p, o_g, o_m, o_s, n_p, n_g, n_m, n_s) = refs[:16]
    (qk_new, qk_first, qk_second, vg_new, vg_first, vg_second, o_new, o_first, o_second,
     n_new, n_first, n_second, part_a, part_b, o_copy, n_copy) = refs[16:32]
    (b_qk, b_vg, b_o, b_n, u_qk, u_vg, u_o, slots_one, slots_two, load_sem, one_send, one_recv, two_send, two_recv,
     ax_send, ax_recv, bz_send, bz_recv, bx_send, bx_recv, br_send, br_recv, az_send, az_recv) = refs[32:]

    shard = lax.axis_index("shard")
    y = lax.axis_index("tensor")
    z = shard // NX
    x = shard % NX
    q = y * NX + x

    def at(dz=0, dx=0):
        return {"shard": ((z + dz + NZ) % NZ) * NX + (x + dx + NX) % NX}

    def at_plane(d):
        other = (q + d) % (NX * NY)
        return {"shard": z * NX + other % NX, "tensor": other // NX}

    def rows(dz=0, dx=0):
        return pl.multiple_of(((z + dz + NZ) % NZ) * GROUP + ((x + dx + NX) % NX) * ROWS, ROWS)

    barrier = pltpu.get_barrier_semaphore()
    for d in range(1, NX * NY):
        pl.semaphore_signal(barrier, inc=1, device_id=at_plane(d), device_id_type=MESH)
    for d in range(1, NZ):
        pl.semaphore_signal(barrier, inc=1, device_id=at(dz=d), device_id_type=MESH)

    loads = []
    for i, (group, buffer) in enumerate((
        ((qk_p, qk_g, qk_m, qk_s), b_qk), ((vg_p, vg_g, vg_m, vg_s), b_vg),
        ((o_p, o_g, o_m, o_s), b_o), ((n_p, n_g, n_m, n_s), b_n))):
        for k, ref in enumerate(group):
            loads.append(pltpu.make_async_copy(ref, buffer.at[k], load_sem.at[4 * i + k]))
            loads[-1].start()

    lane = lax.broadcasted_iota(jnp.int32, (1, 128), 1)
    line = jnp.zeros((1, 128), jnp.float32)
    for k in range(4):
        loads[12 + k].wait()
    first, second, gain_update = terms(b_n[0], b_n[1], b_n[2], b_n[3], 0.0)
    n_first[...] = first
    n_second[...] = second
    slots_one[q] = line
    slots_one[q, :, 0:16] = b_n[0]
    slots_one[q, :, 16:32] = gain_update
    index = 0
    for i, (buffer, u_ref, first_ref, second_ref, count) in enumerate((
        (b_qk, u_qk, qk_first, qk_second, 2), (b_vg, u_vg, vg_first, vg_second, 2), (b_o, u_o, o_first, o_second, 1))):
        for k in range(4):
            loads[4 * i + k].wait()
        for k in range(count):
            p, g, m, s = (buffer[j, k] for j in range(4))
            first, second, update = terms(p, g, m, s, 0.01)
            first_ref[k] = first
            second_ref[k] = second
            u_ref[k] = update
            line = jnp.where(lane == W_LANE + index, total(p * p), line)
            line = jnp.where(lane == U_LANE + index, total(update * update), line)
            index += 1
    slots_one[q] = slots_one[q] + line

    pl.semaphore_wait(barrier, NX * NY - 1 + NZ - 1)
    sends = []
    one = []
    for d in range(1, NX * NY):
        one.append(pltpu.make_async_remote_copy(
            slots_one.at[q], slots_one.at[q], one_send.at[d - 1], one_recv.at[d - 1], device_id=at_plane(d), device_id_type=MESH))
        one[-1].start()
    for copy in one:
        copy.wait_recv()
    sends += one
    plane = slots_one[0]
    for d in range(1, NX * NY):
        plane = plane + slots_one[d]
    gains = jnp.zeros((1, 128), jnp.float32)
    for k in range(NX):
        gain_line = jnp.where(lane < 32, slots_one[y * NX + k], 0.0)
        gains = gains + (pltpu.roll(gain_line, 32 * k, 1) if k else gain_line)
    slots_two[z, 0:1] = plane
    slots_two[z, 1:2] = gains
    two = []
    for d in range(1, NZ):
        two.append(pltpu.make_async_remote_copy(
            slots_two.at[z], slots_two.at[z], two_send.at[d - 1], two_recv.at[d - 1], device_id=at(dz=d), device_id_type=MESH))
        two[-1].start()
    for copy in two:
        copy.wait_recv()
    sends += two
    sums = slots_two[0, 0:1]
    for d in range(1, NZ):
        sums = sums + slots_two[d, 0:1]
    roots = jnp.sqrt(jnp.where(lane >= W_LANE, sums, 0.0))
    ratio = LEARN_RATE * (roots / (pltpu.roll(roots, 128 - (U_LANE - W_LANE), 1) + EPSILON))
    rate = [jnp.sum(jnp.where(lane == W_LANE + i, ratio, 0.0), axis=1, keepdims=True) for i in range(5)]

    mine = rows()
    new = b_vg[0, 0] - rate[2] * u_vg[0]
    vg_new[0] = new
    part_b[pl.ds(mine, ROWS), 0:512] = new.astype(jnp.bfloat16)
    new = b_vg[0, 1] - rate[3] * u_vg[1]
    vg_new[1] = new
    part_b[pl.ds(mine, ROWS), 512:1024] = new.astype(jnp.bfloat16)
    new = b_qk[0, 1] - rate[1] * u_qk[1]
    qk_new[1] = new
    part_b[pl.ds(mine, ROWS), 1024:1280] = new.astype(jnp.bfloat16)

    def send(ref, start, size, send_sem, recv_sem, target):
        block = ref.at[pl.ds(start, size)]
        copy = pltpu.make_async_remote_copy(block, block, send_sem, recv_sem, device_id=target, device_id_type=MESH)
        copy.start()
        sends.append(copy)
        return copy

    SIDE = (1, -1)
    STEPS = (HALF, HALF - 1)

    def send_bz(side, k):
        return send(part_b, rows(dz=-SIDE[side] * k), ROWS, bz_send.at[side, k], bz_recv.at[side, k], at(dz=SIDE[side]))

    def send_bx(j, dz):
        return [send(part_b, rows(dz=dz), ROWS, bx_send.at[side, j], bx_recv.at[side, j], at(dx=SIDE[side])) for side in range(2)]

    def relay_bx(j, dz):
        side = j % 2
        across[j][side].wait_recv()
        return send(part_b, rows(dz=dz, dx=-SIDE[side]), ROWS, br_send.at[j], br_recv.at[j], at(dx=SIDE[side]))

    PIECE = GROUP // SUBS

    def subs_of(side, k):
        if k < HALF - 1:
            return range(SUBS)
        return range(SUBS // 2) if side == 0 else range(SUBS // 2, SUBS)

    def send_az(side, k, h):
        dz = -SIDE[side] * k
        start = pl.multiple_of(((z + dz + NZ) % NZ) * GROUP + h * PIECE, PIECE)
        return send(part_a, start, PIECE, az_send.at[side, k, h], az_recv.at[side, k, h], at(dz=SIDE[side]))

    bz = [[send_bz(0, 0)], [send_bz(1, 0)]]
    new = b_o[0, 0] - rate[4] * u_o[0]
    o_new[0] = new
    part_a[pl.ds(mine, ROWS), 0:512] = new.astype(jnp.bfloat16)
    new = b_qk[0, 0] - rate[0] * u_qk[0]
    qk_new[0] = new
    part_a[pl.ds(mine, ROWS), 512:768] = new.astype(jnp.bfloat16)
    ax = [send(part_a, mine, ROWS, ax_send.at[d - 1], ax_recv.at[d - 1], at(dx=d)) for d in (1, 3, 2)]
    across = {0: send_bx(0, 0)}
    relays = {}
    where = {0: 0}

    lanes = lax.broadcasted_iota(jnp.int32, (NZ, 128), 1)
    held = jnp.concatenate([slots_two[d, 1:2] for d in range(NZ)], axis=0)
    valid = lanes % 32 < 16
    gain = jnp.where(valid, held, 0.0)
    update = jnp.where(valid, pltpu.roll(held, 128 - 16, 1), 0.0)
    gain_rate = LEARN_RATE * (jnp.sqrt(total(gain * gain)) / (jnp.sqrt(total(update * update)) + EPSILON))
    n_new[...] = b_n[0] - gain_rate * gain_update
    gain = gain - gain_rate * update
    packed = jnp.where(lanes < 16, gain, 0.0)
    for k in range(1, NX):
        packed = packed + jnp.where((lanes >= 16 * k) & (lanes < 16 * k + 16), pltpu.roll(gain, 128 - 16 * k, 1), 0.0)
    moved = pltpu.roll(packed, 64, 1)
    for d in range(HALF):
        n_copy[:, 128 * d : 128 * d + 128] = (packed[2 * d : 2 * d + 1] + moved[2 * d + 1 : 2 * d + 2]).astype(jnp.bfloat16)

    def transpose_pair(i):
        start = pl.multiple_of((z // 2 + i + HALF) % HALF * 128, 128)
        block = part_a[pl.ds(start, 128), 0:512].astype(jnp.float32)
        o_copy[:, pl.ds(start, 128)] = block.T.astype(jnp.bfloat16)

    az = [{}, {}]

    def az_step(k):
        if k == 0:
            for copy in ax:
                copy.wait_recv()
        for h in range(SUBS):
            for side in range(2):
                if k:
                    if h in subs_of(side, k - 1):
                        az[side][k - 1, h].wait_recv()
                if k < HALF and h in subs_of(side, k):
                    az[side][k, h] = send_az(side, k, h)
        if k == HALF:
            transpose_pair(HALF // 2)
        elif k % 2 == 1:
            i = (k - 1) // 2
            transpose_pair(-i)
            if i:
                transpose_pair(i)

    for k in range(HALF + max(LAG, 1) + 1):
        if k < HALF:
            for side in range(2):
                if k < STEPS[side]:
                    bz[side][k].wait_recv()
                    if k + 1 < STEPS[side]:
                        bz[side].append(send_bz(side, k + 1))
                    j = 1 + 2 * k + side
                    where[j] = -SIDE[side] * (k + 1)
                    across[j] = send_bx(j, where[j])
        if k >= LAG and k - LAG <= HALF:
            az_step(k - LAG)
        for j in ((0,) if k == 0 else (2 * k - 1, 2 * k)):
            if j < NZ:
                relays[j] = relay_bx(j, where[j])
    for j in range(NZ):
        across[j][1 - j % 2].wait_recv()
        relays[j].wait_recv()
    for copy in sends:
        copy.wait_send()


def store_kernel(*refs):
    (qk_new, qk_first, qk_second, vg_new, vg_first, vg_second, o_new, o_first, o_second,
     n_new, n_first, n_second, part_a, part_b, o_copy, n_copy) = refs[:16]
    outs = refs[16:32]
    sem = refs[32]
    pairs = [
        (part_b.at[:, 0:512], outs[13].at[0]), (part_b.at[:, 512:1024], outs[13].at[1]), (o_copy, outs[14]),
        (part_a.at[:, 512:768], outs[12].at[0]), (part_b.at[:, 1024:1280], outs[12].at[1]),
        *zip(refs[:12], outs[:12]), (n_copy, outs[15])]
    copies = [pltpu.make_async_copy(source, target, sem.at[i]) for i, (source, target) in enumerate(pairs)]
    for copy in copies:
        copy.start()
    for copy in copies:
        copy.wait()


def on_device(*args):
    f32, bf16 = jnp.float32, jnp.bfloat16
    operands = []
    for i, array in enumerate(args):
        if i < 8:
            operands.append(array.reshape(array.shape[1:]))
        elif i < 12:
            operands.append(jnp.swapaxes(array, 1, 2))
        else:
            operands.append(array)
    qk, vg, o, n = (operands[4 * i].shape for i in range(4))
    small = [(qk, f32)] * 3 + [(vg, f32)] * 3 + [(o, f32)] * 3 + [(n, f32)] * 3
    rows = NZ * GROUP
    middle = small + [((rows, A_COLS), bf16), ((rows, B_COLS), bf16), ((512, rows), bf16), ((1, rows), bf16)]
    final = small + [((2, rows, 256), bf16), ((2, rows, 512), bf16), ((512, rows), bf16), ((1, rows), bf16)]
    dma = pltpu.SemaphoreType.DMA
    held = pl.pallas_call(
        comm_kernel,
        out_shape=[jax.ShapeDtypeStruct(*s) for s in middle],
        in_specs=[pl.BlockSpec(memory_space=pl.ANY)] * 16,
        out_specs=[pl.BlockSpec(memory_space=pltpu.VMEM)] * 16,
        scratch_shapes=[
            pltpu.VMEM((4,) + qk, f32), pltpu.VMEM((4,) + vg, f32), pltpu.VMEM((4,) + o, f32), pltpu.VMEM((4,) + n, f32),
            pltpu.VMEM(qk, f32), pltpu.VMEM(vg, f32), pltpu.VMEM(o, f32),
            pltpu.VMEM((NX * NY, 1, 128), f32), pltpu.VMEM((NZ, 2, 128), f32),
            dma((16,)), dma((NX * NY - 1,)), dma((NX * NY - 1,)), dma((NZ - 1,)), dma((NZ - 1,)),
            dma((3,)), dma((3,)), dma((2, HALF)), dma((2, HALF)), dma((2, NZ)), dma((2, NZ)), dma((NZ,)), dma((NZ,)),
            dma((2, HALF, SUBS)), dma((2, HALF, SUBS))],
        compiler_params=pltpu.CompilerParams(collective_id=0, has_side_effects=True, vmem_limit_bytes=24 << 20),
        name="lamb_gather",
    )(*operands)
    outs = pl.pallas_call(
        store_kernel,
        out_shape=[jax.ShapeDtypeStruct(*s) for s in final],
        in_specs=[pl.BlockSpec(memory_space=pltpu.VMEM)] * 16,
        out_specs=[pl.BlockSpec(memory_space=pl.ANY)] * 16,
        scratch_shapes=[dma((18,))],
        compiler_params=pltpu.CompilerParams(vmem_limit_bytes=24 << 20),
        name="store",
    )(*held)
    outs = list(outs)
    for i in (0, 1, 2, 3, 4, 5, 12, 13, 14):
        outs[i] = outs[i][None]
    for i in (6, 7, 8):
        outs[i] = jnp.swapaxes(outs[i], 1, 2)
    return tuple(outs)


def solution(mesh):
    matrix = P("section", None, "shard", "tensor")
    across = P("section", "tensor", "shard")
    gain = P("section", "shard")
    return jax.shard_map(
        on_device,
        mesh=mesh,
        in_specs=(matrix,) * 8 + (across,) * 4 + (gain,) * 4,
        out_specs=(matrix,) * 6 + (across,) * 3 + (gain,) * 3
        + (P("section", None, None, "tensor"), P("section", None, None, "tensor"), P("section", "tensor", None), P("section", None)),
        check_vma=False,
    )
```

time: 1120 us -> 83.6 us (0.07)
  the two profiles are of different devices: /device:TPU:1 before, /device:TPU:6 now
where the time goes in v1:
time: 83.6 us; the launch traced here: 82.7 us
  Pallas kernels  70 us (84%)
  local copies, waits for them, and re-layouts  12 us (14%)
    pallas_call x1, Pallas kernels, on_device(): pl.pallas_call(comm_kernel, out_shape=[jax.ShapeDtypeStruct(*s) for s in...  67.7 us
    unnamed x32, local copies, waits for them, and re-layouts  12 us
    pallas_call x1, Pallas kernels, on_device(): pl.pallas_call(store_kernel, out_shape=[jax.ShapeDtypeStruct(*s) for s in...  2.29 us

profile of v1, /device:TPU:6, one launch (start us, length us, event | category | flops | bytes accessed | tf_op | source)
XLA Modules:
  0.0 82.7 jit_solution(7092423837736443785)
XLA Ops:
  0.7 0.0 copy-start
  0.7 0.8 %copy-done = f32[1,2,16,512]{3,2,1,0:T(8,128)S(1)} copy-done((f32[1,2,16,512]{3,2,1,0:T(8,128)S(1)}, f32[1,2,16,512]{3,2,1,0:T(8,128)}, u32[]{:S(2)}) %copy-start) | copy-done | bytes 65560
  1.5 0.0 copy-start.1
  1.5 0.8 %copy-done.1 = f32[1,2,16,512]{3,2,1,0:T(8,128)S(1)} copy-done((f32[1,2,16,512]{3,2,1,0:T(8,128)S(1)}, f32[1,2,16,512]{3,2,1,0:T(8,128)}, u32[]{:S(2)}) %copy-start.1) | copy-done | bytes 65560
  2.3 0.0 copy-start.2
  2.3 0.8 %copy-done.2 = f32[1,2,16,512]{3,2,1,0:T(8,128)S(1)} copy-done((f32[1,2,16,512]{3,2,1,0:T(8,128)S(1)}, f32[1,2,16,512]{3,2,1,0:T(8,128)}, u32[]{:S(2)}) %copy-start.2) | copy-done | bytes 65560
  3.2 0.0 copy-start.3
  3.2 0.8 %copy-done.3 = f32[1,2,16,512]{3,2,1,0:T(8,128)S(1)} copy-done((f32[1,2,16,512]{3,2,1,0:T(8,128)S(1)}, f32[1,2,16,512]{3,2,1,0:T(8,128)}, u32[]{:S(2)}) %copy-start.3) | copy-done | bytes 65560
  4.0 0.0 copy-start.4
  4.0 0.8 copy-done.4
  4.8 0.0 copy-start.5
  4.8 0.8 copy-done.5
  5.5 0.8 copy-done.6
  6.3 0.8 copy-done.7
  7.0 0.8 copy-done.8
  7.8 0.8 copy-done.9
  8.6 0.8 copy-done.10
  9.3 0.8 copy-done.11
  10.1 0.7 copy-done.12
  10.7 0.7 copy-done.13
  11.4 0.7 copy-done.14
  12.1 0.7 copy-done.15
  12.7 67.7 %lamb_gather.1 = (f32[2,16,256]{2,1,0:T(8,128)S(1)}, f32[2,16,256]{2,1,0:T(8,128)S(1)}, f32[2,16,256]{2,1,0:T(8,128)S(1)}, f32[2,16,512]{2,1,0:T(8,128)S(1)}, f3...) custom-call(f32[2,16,256]{2,1,0:T(8,128)S(1)} %bitcast.28, ...), custom_call_target="tpu_custom_call" | custom-call | tf_op jit(solution)/shard_map/lamb_gather/pallas_call | solution.py:290
  80.4 2.3 %store.1 = (f32[2,16,256]{2,1,0:T(8,128)}, f32[2,16,256]{2,1,0:T(8,128)}, f32[2,16,256]{2,1,0:T(8,128)}, f32[2,16,512]{2,1,0:T(8,128)}, f32[2,16,512]{2,1,0:T(8,...) custom-call(f32[2,16,256]{2,1,0:T(8,128)S(1)} %get-tuple-element.48., ...), custom_call_target="tpu_custom_call" | custom-call | tf_op jit(solution)/shard_map/store/pallas_call | solution.py:305
  (10 shorter events, 0.0 us)
Async XLA Ops:
  0.7 0.8 %copy-start = (f32[1,2,16,512]{3,2,1,0:T(8,128)S(1)}, f32[1,2,16,512]{3,2,1,0:T(8,128)}, u32[]{:S(2)}) copy-start(f32[1,2,16,512]{3,2,1,0:T(8,128)} %param.20) | copy-start | bytes 196612
  1.5 0.8 %copy-start.1 = (f32[1,2,16,512]{3,2,1,0:T(8,128)S(1)}, f32[1,2,16,512]{3,2,1,0:T(8,128)}, u32[]{:S(2)}) copy-start(f32[1,2,16,512]{3,2,1,0:T(8,128)} %param.21) | copy-start | bytes 196612
  2.3 0.8 %copy-start.2 = (f32[1,2,16,512]{3,2,1,0:T(8,128)S(1)}, f32[1,2,16,512]{3,2,1,0:T(8,128)}, u32[]{:S(2)}) copy-start(f32[1,2,16,512]{3,2,1,0:T(8,128)} %param.22) | copy-start | bytes 196612
  3.2 0.8 %copy-start.3 = (f32[1,2,16,512]{3,2,1,0:T(8,128)S(1)}, f32[1,2,16,512]{3,2,1,0:T(8,128)}, u32[]{:S(2)}) copy-start(f32[1,2,16,512]{3,2,1,0:T(8,128)} %param.23) | copy-start | bytes 196612
  4.0 0.8 copy-start.4
  4.8 0.8 copy-start.5
  5.5 0.8 copy-start.6
  6.3 0.8 copy-start.7
  7.0 0.8 copy-start.8
  7.8 0.8 copy-start.9
  8.6 0.8 copy-start.10
  9.3 0.8 copy-start.11
  10.1 0.7 copy-start.12
  10.7 0.7 copy-start.13
  11.4 0.7 copy-start.14
  12.0 0.7 copy-start.15

commit v2 on v1

--- a/solution.py
+++ b/solution.py
@@ -23,6 +23,7 @@
 A_COLS, B_COLS = 768, 1280
 SUBS = 4
 W_LANE, U_LANE = 64, 72
+FAR_FIRST = sorted(range(1, NZ), key=lambda d: -min(d, NZ - d))
 LAG = 1
 
 
@@ -63,10 +64,10 @@
         return pl.multiple_of(((z + dz + NZ) % NZ) * GROUP + ((x + dx + NX) % NX) * ROWS, ROWS)
 
     barrier = pltpu.get_barrier_semaphore()
+    for d in FAR_FIRST:
+        pl.semaphore_signal(barrier, inc=1, device_id=at(dz=d), device_id_type=MESH)
     for d in range(1, NX * NY):
         pl.semaphore_signal(barrier, inc=1, device_id=at_plane(d), device_id_type=MESH)
-    for d in range(1, NZ):
-        pl.semaphore_signal(barrier, inc=1, device_id=at(dz=d), device_id_type=MESH)
 
     loads = []
     for i, (group, buffer) in enumerate((
@@ -122,7 +123,7 @@
     slots_two[z, 0:1] = plane
     slots_two[z, 1:2] = gains
     two = []
-    for d in range(1, NZ):
+    for d in FAR_FIRST:
         two.append(pltpu.make_async_remote_copy(
             slots_two.at[z], slots_two.at[z], two_send.at[d - 1], two_recv.at[d - 1], device_id=at(dz=d), device_id_type=MESH))
         two[-1].start()
@@ -301,7 +302,7 @@
             dma((2, HALF, SUBS)), dma((2, HALF, SUBS))],
         compiler_params=pltpu.CompilerParams(collective_id=0, has_side_effects=True, vmem_limit_bytes=24 << 20),
         name="lamb_gather",
-    )(*operands)
+    )(*[pltpu.with_memory_space_constraint(a, pltpu.HBM) for a in operands])
     outs = pl.pallas_call(
         store_kernel,
         out_shape=[jax.ShapeDtypeStruct(*s) for s in final],

time: 83.6 us -> 70.5 us (0.84)
  local copies, waits for them, and re-layouts: 12 us -> 0 us
    unnamed x32 -> x0, local copies, waits for them, and re-layouts: 12 us -> none
where the time goes in v2:
time: 70.5 us; the launch traced here: 70.3 us
  Pallas kernels  69.6 us (99%)
    pallas_call x1, Pallas kernels, on_device(): pl.pallas_call(comm_kernel, out_shape=[jax.ShapeDtypeStruct(*s) for s in...  67.3 us
    pallas_call x1, Pallas kernels, on_device(): pl.pallas_call(store_kernel, out_shape=[jax.ShapeDtypeStruct(*s) for s in...  2.29 us

profile of v2, /device:TPU:6, one launch (start us, length us, event | category | flops | bytes accessed | tf_op | source)
XLA Modules:
  0.0 70.3 jit_solution(6890202672030192303)
XLA Ops:
  0.7 67.3 %lamb_gather.1 = (f32[2,16,256]{2,1,0:T(8,128)S(1)}, f32[2,16,256]{2,1,0:T(8,128)S(1)}, f32[2,16,256]{2,1,0:T(8,128)S(1)}, f32[2,16,512]{2,1,0:T(8,128)S(1)}, f3...) custom-call(f32[2,16,256]{2,1,0:T(8,128)} %bitcast.28, ...), custom_call_target="tpu_custom_call" | custom-call | tf_op jit(solution)/shard_map/lamb_gather/pallas_call | solution.py:291
  68.0 2.3 %store.1 = (f32[2,16,256]{2,1,0:T(8,128)}, f32[2,16,256]{2,1,0:T(8,128)}, f32[2,16,256]{2,1,0:T(8,128)}, f32[2,16,512]{2,1,0:T(8,128)}, f32[2,16,512]{2,1,0:T(8,...) custom-call(f32[2,16,256]{2,1,0:T(8,128)S(1)} %get-tuple-element.48., ...), custom_call_target="tpu_custom_call" | custom-call | tf_op jit(solution)/shard_map/store/pallas_call | solution.py:306
